TPU v7x, 32 devices: a whole 2x2x4 slice. The times are simulated.
32 devices in a mesh: groups: 2 (over x), frames: 16 (over z, y, core).
Axes of the slice: x: 2, y: 2, z: 4, core: 2. Of those that a mesh axis runs over, the one named last changes fastest.
Arguments:
- video: float32 [4, 16, 256, 256], P('groups', 'frames'), parts along dimension 0, may hold values from -9 to 9
- clip_start: int32 [4], P('groups'), parts along dimension 0, may hold values from 0 to 7
- gain_space: float32 [256], replicated, may hold values from 0.1 to 1.9
- qkv_space: float32 [256, 768], replicated, may hold values from -0.375 to 0.375
- out_space: float32 [256, 256], replicated, may hold values from -0.375 to 0.375
- gain_time: float32 [256], replicated, may hold values from 0.1 to 1.9
- qkv_time: float32 [256, 768], replicated, may hold values from -0.375 to 0.375
- out_time: float32 [256, 256], replicated, may hold values from -0.375 to 0.375
- code_sums: float32 [8192, 256], P(('groups', 'frames')), parts along dimension 0, may hold values from -12 to 12
- code_counts: float32 [8192], P(('groups', 'frames')), parts along dimension 0, may hold values from 1 to 10
Outputs:
- latents: float32 [4, 16, 256, 256], P('groups', None, 'frames'), parts along dimension 0
- new_sums: float32 [8192, 256], P(('groups', 'frames')), parts along dimension 0
- new_counts: float32 [8192], P(('groups', 'frames')), parts along dimension 0
- new_codebook: float32 [8192, 256], P(('groups', 'frames')), parts along dimension 0
There are 2 independent parts, one for each index of `groups`. A program takes and returns all parts, laid end to end along the dimension named above; an argument that names none is the same for every part. Nothing has to cross between parts.
All inputs are finite; a program needn't handle non-finite values.
Results may differ from a plain program's by a relative error of at most 0.0003.
Values sent between devices are 32-bit elements; how exact they have to be, the bound alone decides.
A program may use at most 64 MiB of HBM per device.

v0:
```python
import jax
import jax.numpy as jnp
from jax import lax
from jax.sharding import PartitionSpec as P

HEADS = 4
ATTN_SCALE = 10.0
SOFTMAX_WARMTH = 0.05
DECAY_RATE = 0.9
EPSILON = 1e-06
TOP_PRECISION = lax.Precision.HIGHEST


def rms_norm(values, gain_vec):
    return values * lax.rsqrt(jnp.mean(values * values, -1, keepdims=True) + EPSILON) * gain_vec


def unit_vec(values):
    return values * lax.rsqrt(jnp.sum(values * values, -1, keepdims=True) + EPSILON)


def spatial_block(one_frame, gain_vec, w_qkv, w_out):
    width = one_frame.shape[-1]
    normed = rms_norm(one_frame, gain_vec)
    packed = jnp.dot(normed, w_qkv, precision=TOP_PRECISION)
    queries = unit_vec(packed[:, :width].reshape(-1, HEADS, width // HEADS))
    key_vecs = unit_vec(packed[:, width : 2 * width].reshape(-1, HEADS, width // HEADS))
    values = packed[:, 2 * width :].reshape(-1, HEADS, width // HEADS)
    scores = ATTN_SCALE * jnp.einsum("qhd,khd->hqk", queries, key_vecs, precision=TOP_PRECISION)
    assignment_weights = jnp.exp(scores)
    totals = jnp.sum(assignment_weights, -1).T[:, :, None]
    mixed = jnp.einsum("hqk,khd->qhd", assignment_weights, values, precision=TOP_PRECISION) / totals
    return one_frame + jnp.dot(mixed.reshape(-1, width), w_out, precision=TOP_PRECISION)


def time_block(spaced, clip_start, gain_vec, w_qkv, w_out):
    clips, frames, places, width = spaced.shape
    normed = rms_norm(spaced, gain_vec)
    packed = jnp.einsum("ctpd,de->ctpe", normed, w_qkv, precision=TOP_PRECISION)
    shape_heads = (clips, frames, places, HEADS, width // HEADS)
    queries = unit_vec(packed[..., :width].reshape(shape_heads))
    key_vecs = unit_vec(packed[..., width : 2 * width].reshape(shape_heads))
    values = packed[..., 2 * width :].reshape(shape_heads)
    scores = ATTN_SCALE * jnp.einsum(
        "ctphd,csphd->cphts", queries, key_vecs, precision=TOP_PRECISION
    )
    later = jnp.arange(frames, dtype=jnp.int32)[:, None]
    earlier = jnp.arange(frames, dtype=jnp.int32)[None, :]
    allowed = (earlier <= later)[None] & (
        (earlier[None] >= clip_start[:, None, None]) | (earlier == later)[None]
    )
    assignment_weights = jnp.exp(scores) * allowed[:, None, None, :, :].astype(jnp.float32)
    totals = jnp.transpose(jnp.sum(assignment_weights, -1), (0, 3, 1, 2))[..., None]
    mixed = (
        jnp.einsum("cphts,csphd->ctphd", assignment_weights, values, precision=TOP_PRECISION)
        / totals
    )
    return spaced + jnp.einsum(
        "ctpd,de->ctpe", mixed.reshape(clips, frames, places, width), w_out, precision=TOP_PRECISION
    )


def local(
    video,
    clip_start,
    gain_space,
    qkv_space,
    out_space,
    gain_time,
    qkv_time,
    out_time,
    code_sums,
    code_counts,
):
    clips, local_frames, places, width = video.shape
    flat_frames = video.reshape(clips * local_frames, places, width)
    spaced = lax.map(
        lambda one_frame: spatial_block(one_frame, gain_space, qkv_space, out_space), flat_frames
    )
    spaced = spaced.reshape(clips, local_frames, places, width)
    by_place = lax.all_to_all(spaced, "frames", split_axis=2, concat_axis=1, tiled=True)
    latents = time_block(by_place, clip_start, gain_time, qkv_time, out_time)
    unit_token_vectors = unit_vec(latents.reshape(-1, width))
    local_codes = unit_vec(code_sums / code_counts[:, None])
    codebook_matrix = lax.all_gather(local_codes, "frames", axis=0, tiled=True)
    assignment_weights = jnp.exp(
        jnp.dot(unit_token_vectors, codebook_matrix.T, precision=TOP_PRECISION) / SOFTMAX_WARMTH
    )
    probs = assignment_weights / jnp.sum(assignment_weights, 1, keepdims=True)
    term_sums = lax.dot_general(
        probs, unit_token_vectors, (((0,), (0,)), ((), ())), precision=TOP_PRECISION
    )
    term_counts = jnp.sum(probs, 0)
    got_sums, got_counts = (
        lax.psum_scatter(term_sums, "frames", scatter_dimension=0, tiled=True),
        lax.psum_scatter(term_counts, "frames", scatter_dimension=0, tiled=True),
    )
    new_sums = DECAY_RATE * code_sums + (1.0 - DECAY_RATE) * got_sums
    new_counts = DECAY_RATE * code_counts + (1.0 - DECAY_RATE) * got_counts
    new_codebook = new_sums / new_counts[:, None]
    return (latents, new_sums, new_counts, new_codebook)


def solution(mesh):
    in_specs = (
        P("groups", "frames", None, None),
        P("groups"),
        P(),
        P(),
        P(),
        P(),
        P(),
        P(),
        P(("groups", "frames"), None),
        P(("groups", "frames")),
    )
    out_specs = (
        P("groups", None, "frames", None),
        P(("groups", "frames"), None),
        P(("groups", "frames")),
        P(("groups", "frames"), None),
    )
    return jax.shard_map(local, mesh=mesh, in_specs=in_specs, out_specs=out_specs, check_vma=False)
```

profile of v0, /device:TPU:0, one launch (start us, length us, event | category | flops | bytes accessed | tf_op | source)
XLA Modules:
  0.0 198.9 jit_solution(9034979632726046601)
XLA Ops:
  7.2 1.2 multiply_reduce_fusion.6
  8.4 1.8 broadcast_multiply_fusion.2
  10.3 25.9 %while.10 = (s32[]{:T(128)}, f32[2,256,256]{2,0,1:T(2,128)}, f32[2,256,256]{2,1,0:T(8,128)}, f32[256]{0:T(256)}, f32[256,768]{1,0:T(8,128)}, /*index=5*/f32[256,256]{1,0:T(8,128)}, s32[]{:T(128)}, s32[]{:T(128)}) while((s32[]{:T(128)}, f32[2,256,256]{2,0,1:T(2,128)}, f32[2,256,256]{2,1,0:T(8,128)}, f32[256]{0:T(256)}, f32[256,768]{1,0:T(8,128)}, ...), condition=%wide.region_5.6_spmd, body=%wide.region_0.5_spmd.sunk | while | flops 1209269504 | bytes 14202521 | solution.py:77
  10.3 1.1 fusion.67
  11.5 2.1 %fusion.68 = f32[256,768]{1,0:T(8,128)S(1)} fusion(f32[256,768]{1,0:T(8,128)} %get-tuple-element.142, f32[2,256,256]{2,1,0:T(8,128)} %get-tuple-element.140, s32[]{:T(128)} %get-tuple-element.130, f32[256]{0:T(256)} %get-tuple-element.141, f32[256]{0:T(256)S(1)} %add_rsqrt_fusion.10), kind=kOutput, calls=%fused_computation.10.clone.1 | convolution fusion | flops 604110848 | bytes 1837568 | tf_op jit(solution)/shard_map/while/body/eval_jaxpr/dot_general | solution.py:25
  13.6 0.1 copy.84
  13.8 0.1 copy.83
  14.0 1.1 fusion.70
  15.1 0.1 copy.82
  15.3 0.8 fusion.71
  16.1 0.6 fusion.72
  16.7 0.3 copy.85
  16.9 6.3 %dynamic_update_slice.5 = f32[2,256,256]{2,0,1:T(2,128)} dynamic-update-slice(f32[2,256,256]{2,0,1:T(2,128)} %get-tuple-element.131, f32[1,256,256]{2,0,1:T(1,128)S(1)} %copy.85, s32[]{:T(128)} %get-tuple-element.130, s32[]{:T(128)} %constant.22.clone.1..sunk, s32[]{:T(128)} %constant.22.clone.1..sunk) | dynamic-update-slice | bytes 524292 | tf_op jit(solution)/shard_map/while/body/jit(dynamic_update_index_in_dim)/dynamic_update_slice | solution.py:77
  23.3 1.1 fusion.67
  24.4 2.1 %fusion.68 = f32[256,768]{1,0:T(8,128)S(1)} fusion(f32[256,768]{1,0:T(8,128)} %get-tuple-element.142, f32[2,256,256]{2,1,0:T(8,128)} %get-tuple-element.140, s32[]{:T(128)} %get-tuple-element.130, f32[256]{0:T(256)} %get-tuple-element.141, f32[256]{0:T(256)S(1)} %add_rsqrt_fusion.10), kind=kOutput, calls=%fused_computation.10.clone.1 | convolution fusion | flops 604110848 | bytes 1837568 | tf_op jit(solution)/shard_map/while/body/eval_jaxpr/dot_general | solution.py:25
  26.6 0.1 copy.84
  26.7 0.1 copy.83
  26.9 1.1 fusion.70
  28.2 0.8 fusion.71
  29.0 0.6 fusion.72
  29.6 0.3 copy.85
  29.9 6.3 %dynamic_update_slice.5 = f32[2,256,256]{2,0,1:T(2,128)} dynamic-update-slice(f32[2,256,256]{2,0,1:T(2,128)} %get-tuple-element.131, f32[1,256,256]{2,0,1:T(1,128)S(1)} %copy.85, s32[]{:T(128)} %get-tuple-element.130, s32[]{:T(128)} %constant.22.clone.1..sunk, s32[]{:T(128)} %constant.22.clone.1..sunk) | dynamic-update-slice | bytes 524292 | tf_op jit(solution)/shard_map/while/body/jit(dynamic_update_index_in_dim)/dynamic_update_slice | solution.py:77
  36.2 7.4 %all-to-all-start = ((f32[2,1,256,256]{3,0,1,2:T(2,128)}), f32[2,1,256,256]{3,0,1,2:T(2,128)S(1)}, u32[]{:S(2)}, u32[]{:S(2)}) async-start(f32[2,1,256,256]{3,0,1,2:T(2,128)} %bitcast.103), calls=%async_computation | async-start | bytes 1048576 | tf_op jit(solution)/shard_map/all_to_all | solution.py:81
  43.8 22.8 %all-to-all-done = f32[2,1,256,256]{3,0,1,2:T(2,128)S(1)} async-done(((f32[2,1,256,256]{3,0,1,2:T(2,128)}), f32[2,1,256,256]{3,0,1,2:T(2,128)S(1)}, u32[]{:S(2)}, u32[]{:S(2)}) %all-to-all-start) | async-done | bytes 524320 | tf_op jit(solution)/shard_map/all_to_all | solution.py:81
  66.7 0.3 multiply_reduce_fusion.5
  67.1 0.1 copy.48
  67.3 1.5 fusion.23
  68.8 1.2 fusion.37
  69.9 0.5 reshape.172
  70.4 1.5 reshape.171
  71.9 2.5 %reshape.170 = f32[2,16,16,4,64]{4,3,2,1,0:T(4,128)} reshape(f32[2,16,16,256]{3,2,1,0:T(8,128)} %get-tuple-element.58) | data formatting | bytes 1048576 | tf_op jit(solution)/shard_map/reshape | solution.py:43
  74.3 0.6 multiply_reduce_fusion.2
  74.9 0.6 multiply_reduce_fusion.3
  75.7 1.5 broadcast_multiply_fusion
  77.1 3.1 %fusion.38 = (f32[2,16,4,16]{3,2,1,0:T(4,128)S(1)}, f32[2,16,4,16,16]{3,4,2,1,0:T(8,128)S(1)}) fusion(f32[2,16,16]{1,2,0:T(8,128)S(1)} %and_convert_fusion, f32[2,16,16,4,64]{4,3,2,1,0:T(4,128)S(1)} %get-tuple-element.69, f32[2,16,16,4,64]{4,3,2,1,0:T(4,128)S(1)} %get-tuple-element.70), kind=kOutput, calls=%fused_computation.72 | convolution fusion | flops 25262080 | bytes 1189888 | tf_op jit(solution)/shard_map/ctphd,csphd->cphts/dot_general | solution.py:44
  80.3 2.5 %fusion.17 = f32[2,16,16,4,64]{4,1,3,2,0:T(8,128)S(1)} fusion(f32[2,16,4,16,16]{3,4,2,1,0:T(8,128)S(1)} %get-tuple-element.62, f32[2,16,16,4,64]{4,3,2,1,0:T(4,128)S(1)} %copy-done.6, f32[2,16,16,4]{1,3,2,0:T(4,128)S(1)} %bitcast.106), kind=kOutput, calls=%fused_computation.28 | convolution fusion | flops 25296896 | bytes 1187840 | tf_op jit(solution)/shard_map/cphts,csphd->ctphd/dot_general | solution.py:55
  82.8 0.4 copy.53
  83.3 0.6 reshape.173
  83.9 1.6 multiply_reduce_fusion.4
  85.6 0.1 bitcast_multiply_fusion.2
  85.8 9.9 %fusion.16 = (f32[512]{0:T(512)S(1)}, f32[512,4096]{1,0:T(8,128)S(1)}) fusion(f32[512,256]{1,0:T(8,128)S(1)} %bitcast_multiply_fusion.2, f32[4096,256]{1,0:T(8,128)} %all-gather.2.cloned.1.call-done), kind=kOutput, calls=%fused_computation.26 | convolution fusion | flops 6446644736 | bytes 13109248 | tf_op jit(solution)/shard_map/dot_general | solution.py:87
  95.7 3.2 %copy-done.1 = f32[512,4096]{1,0:T(8,128)} copy-done((f32[512,4096]{1,0:T(8,128)}, f32[512,4096]{1,0:T(8,128)S(1)}, u32[]{:S(2)}) %copy-start.1) | copy-done | bytes 8388632
  98.9 15.0 %fusion.28 = f32[4096,256]{1,0:T(8,128)} fusion(f32[512,256]{1,0:T(8,128)S(1)} %bitcast_multiply_fusion.2, f32[512,4096]{1,0:T(8,128)S(1)} %get-tuple-element.66, f32[512]{0:T(512)S(1)} %get-tuple-element.65), kind=kOutput, calls=%fused_computation.48 | convolution fusion | flops 6446645248 | bytes 13109248 | tf_op jit(solution)/shard_map/dot_general | solution.py:90
  114.0 0.6 dynamic-slice
  115.2 4.3 %fusion.27 = f32[4096]{0:T(1024)S(1)} fusion(f32[512]{0:T(512)S(1)} %get-tuple-element.65, f32[512,4096]{1,0:T(8,128)} %copy-done.1), kind=kLoop, calls=%fused_computation.47 | loop fusion | flops 6287360 | bytes 8407040 | tf_op jit(solution)/shard_map/reduce_sum | solution.py:93
  119.5 64.5 %all-reduce = f32[4096]{0:T(1024)S(1)} all-reduce(f32[4096]{0:T(1024)S(1)} %fusion.27), channel_id=3, replica_groups=mesh['groups'=2,'frames'=16] {'frames'}, use_global_device_ids=true, to_apply=%region_15.16.clone | all-reduce | flops 4096 | bytes 32768
  184.1 6.2 %reduce-scatter.2.cloned.1.call-done = f32[256,256]{1,0:T(8,128)} async-done(((f32[4096,256]{1,0:T(8,128)}), f32[256,256]{1,0:T(8,128)}) %reduce-scatter.2.cloned.1.call-update) | async-done | bytes 262160 | tf_op jit(solution)/shard_map/reduce_scatter | solution.py:95
  190.3 1.8 broadcast_divide_fusion
  (55 shorter events, 1.1 us)
Async XLA Ops:
  7.2 60.1 %copy-start = (f32[256,768]{1,0:T(8,128)S(1)}, f32[256,768]{1,0:T(8,128)}, u32[]{:S(2)}) copy-start(f32[256,768]{1,0:T(8,128)} %param.18) | copy-start | bytes 2359300
  7.2 78.6 %all-gather.2.cloned.1.call-start = ((), (), s32[]{:S(2)}) async-start(), calls=%async_computation.2 | async-start | bytes 4456448 | tf_op jit(solution)/shard_map/all_gather | solution.py:85
  10.3 33.4 %copy-start.10 = (s32[2]{0:T(128)S(1)}, s32[2]{0:T(128)}, u32[]{:S(2)}) copy-start(s32[2]{0:T(128)} %param.13) | copy-start | bytes 28
  10.3 57.0 %copy-start.9 = (f32[256]{0:T(256)S(1)}, f32[256]{0:T(256)}, u32[]{:S(2)}) copy-start(f32[256]{0:T(256)} %param.17) | copy-start | bytes 3076
  10.3 5.7 %copy-start.2 = (f32[2,256,256]{2,1,0:T(8,128)S(1)}, f32[2,256,256]{2,1,0:T(8,128)}, u32[]{:S(2)}) copy-start(f32[2,256,256]{2,1,0:T(8,128)} %get-tuple-element.140) | copy-start | bytes 1572868 | tf_op jit(solution)/shard_map/while
  10.3 5.7 %copy-start.3 = (f32[256,256]{1,0:T(8,128)S(1)}, f32[256,256]{1,0:T(8,128)}, u32[]{:S(2)}) copy-start(f32[256,256]{1,0:T(8,128)} %get-tuple-element.143) | copy-start | bytes 786436 | tf_op jit(solution)/shard_map/while
  23.3 5.7 %copy-start.2 = (f32[2,256,256]{2,1,0:T(8,128)S(1)}, f32[2,256,256]{2,1,0:T(8,128)}, u32[]{:S(2)}) copy-start(f32[2,256,256]{2,1,0:T(8,128)} %get-tuple-element.140) | copy-start | bytes 1572868 | tf_op jit(solution)/shard_map/while
  23.3 5.7 %copy-start.3 = (f32[256,256]{1,0:T(8,128)S(1)}, f32[256,256]{1,0:T(8,128)}, u32[]{:S(2)}) copy-start(f32[256,256]{1,0:T(8,128)} %get-tuple-element.143) | copy-start | bytes 786436 | tf_op jit(solution)/shard_map/while
  36.2 30.5 %all-to-all-start = ((f32[2,1,256,256]{3,0,1,2:T(2,128)}), f32[2,1,256,256]{3,0,1,2:T(2,128)S(1)}, u32[]{:S(2)}, u32[]{:S(2)}) async-start(f32[2,1,256,256]{3,0,1,2:T(2,128)} %bitcast.103), calls=%async_computation | async-start | bytes 1048576 | tf_op jit(solution)/shard_map/all_to_all | solution.py:81
  43.6 146.7 %reduce-scatter.2.cloned.1.call-start = ((), (), s32[]{:S(2)}) async-start(), calls=%async_computation.3 | async-start | bytes 4456448 | tf_op jit(solution)/shard_map/reduce_scatter | solution.py:95
  74.3 6.0 %copy-start.6 = (f32[2,16,16,4,64]{4,3,2,1,0:T(4,128)S(1)}, f32[2,16,16,4,64]{4,3,2,1,0:T(4,128)}, u32[]{:S(2)}) copy-start(f32[2,16,16,4,64]{4,3,2,1,0:T(4,128)} %reshape.170) | copy-start | bytes 1572868
  85.5 28.5 %copy-start.5 = (f32[2,16,16,256]{3,2,1,0:T(8,128)}, f32[2,16,16,256]{3,2,1,0:T(8,128)S(1)}, u32[]{:S(2)}) copy-start(f32[2,16,16,256]{3,2,1,0:T(8,128)S(1)} %get-tuple-element.64) | copy-start | bytes 1572868
  95.7 3.2 %copy-start.1 = (f32[512,4096]{1,0:T(8,128)}, f32[512,4096]{1,0:T(8,128)S(1)}, u32[]{:S(2)}) copy-start(f32[512,4096]{1,0:T(8,128)S(1)} %get-tuple-element.66) | copy-start | bytes 25165828
  98.9 15.1 %copy-start.11 = (u32[32]{0:T(128)S(1)}, u32[32]{0:T(128)}, u32[]{:S(2)}) copy-start(u32[32]{0:T(128)} %constant.46) | copy-start | bytes 388
  114.0 70.1 %copy-start.7 = (f32[256]{0:T(256)S(1)}, f32[256]{0:T(256)}, u32[]{:S(2)}) copy-start(f32[256]{0:T(256)} %param.21) | copy-start | bytes 3076
  114.0 76.3 %copy-start.4 = (f32[256,256]{1,0:T(8,128)S(1)}, f32[256,256]{1,0:T(8,128)}, u32[]{:S(2)}) copy-start(f32[256,256]{1,0:T(8,128)} %param.20) | copy-start | bytes 786436
  184.1 8.0 %copy-start.8 = (f32[256]{0:T(256)}, f32[256]{0:T(256)S(1)}, u32[]{:S(2)}) copy-start(f32[256]{0:T(256)S(1)} %fusion.33) | copy-start | bytes 3076
Sparse Core Ops, SparseCore 0:
  10.7 62.2 all-gather.1
  114.1 76.1 reduce-scatter.1
where the time goes:
time: 200 us; the launch traced here: 199 us
  blocking collectives  64.5 us (32%)
  matrix products  42.9 us (21%)
  waiting for transfers between devices  29.1 us (15%)
  local copies, waits for them, and re-layouts  24.8 us (12%)
  other arithmetic  15 us (8%)
  between operations  14.9 us (7%)
  starting transfers between devices  7.5 us (4%)
    unnamed x1, blocking collectives  64.5 us
    all_to_all x1, waiting for transfers between devices, local(): lax.all_to_all(spaced, 'frames', split_axis=2, concat_axis=1, tiled=True)  22.8 us
    dot_general x1, matrix products, local(): lax.dot_general(probs, unit_token_vectors, (((0,), (0,)), ((), ())), prec...  15 us
    dynamic_update_slice x4, local copies, waits for them, and re-layouts, local(): lax.map(lambda one_frame: spatial_block(one_frame, gain_space, qkv_space,...  13.2 us
    dot_general x1, matrix products, local(): jnp.dot(unit_token_vectors, codebook_matrix.T, precision=TOP_PRECISION)  9.91 us
    all_to_all x1, starting transfers between devices, local(): lax.all_to_all(spaced, 'frames', split_axis=2, concat_axis=1, tiled=True)  7.42 us
    reduce_scatter x1, waiting for transfers between devices, local(): lax.psum_scatter(term_sums, 'frames', scatter_dimension=0, tiled=True)  6.17 us
    reduce_sum x1, other arithmetic, local(): term_counts = jnp.sum(probs, 0)  4.27 us
  transfers between devices with their start and end apart: 3, of which 2 were waited for; matrix products, arithmetic and copies ran while one was open for 25% of the time, Pallas kernels for 0%

commit v1 on v0

--- a/solution.py
+++ b/solution.py
@@ -9,6 +9,17 @@
 DECAY_RATE = 0.9
 EPSILON = 1e-06
 TOP_PRECISION = lax.Precision.HIGHEST
+
+
+def in_blocks(shard, dim, length):
+    before, after = (shard.shape[:dim], shard.shape[dim + 1 :])
+    return jnp.moveaxis(shard.reshape(*before, length, -1, *after), dim, 0)
+
+
+def joined_along(pieces, dim):
+    shape = list(pieces.shape[1:])
+    shape[dim] *= pieces.shape[0]
+    return jnp.moveaxis(pieces, 0, dim).reshape(shape)
 
 
 def rms_norm(values, gain_vec):
@@ -78,7 +89,14 @@
         lambda one_frame: spatial_block(one_frame, gain_space, qkv_space, out_space), flat_frames
     )
     spaced = spaced.reshape(clips, local_frames, places, width)
-    by_place = lax.all_to_all(spaced, "frames", split_axis=2, concat_axis=1, tiled=True)
+    count, index = (lax.axis_size("frames"), lax.axis_index("frames"))
+    blocks = in_blocks(spaced, 2, count)
+    outs = [blocks[index]]
+    for hop in range(1, count):
+        sent = blocks[index ^ hop]
+        outs.append(lax.ppermute(sent, "frames", [(i, i ^ hop) for i in range(count)]))
+    blocks = jnp.stack(outs)[index ^ jnp.arange(count)]
+    by_place = joined_along(blocks, 1)
     latents = time_block(by_place, clip_start, gain_time, qkv_time, out_time)
     unit_token_vectors = unit_vec(latents.reshape(-1, width))
     local_codes = unit_vec(code_sums / code_counts[:, None])

time: 200 us -> 190 us (0.950)
  starting transfers between devices: 7.5 us -> 23.6 us
  waiting for transfers between devices: 29.1 us -> 18.2 us
  local copies, waits for them, and re-layouts: 24.8 us -> 13.9 us
  blocking collectives: 64.5 us -> 59.9 us
    ppermute x0 -> x15, starting transfers between devices: none -> 23.5 us  [local(): lax.ppermute(sent, 'frames', [(i, i ^ hop) for i in range(count)])]
    all_to_all x1 -> x0, waiting for transfers between devices: 22.8 us -> none  [local(): lax.all_to_all(spaced, 'frames', split_axis=2, concat_axis=1, tiled=True)]
    dynamic_update_slice x4 -> x0, local copies, waits for them, and re-layouts: 13.2 us -> none  [local(): lax.map(lambda one_frame: spatial_block(one_frame, gain_space, qkv_space,...]
    all_to_all x1 -> x0, starting transfers between devices: 7.42 us -> none  [local(): lax.all_to_all(spaced, 'frames', split_axis=2, concat_axis=1, tiled=True)]
    reduce_scatter x1, waiting for transfers between devices: 6.17 us -> 12.4 us  [local(): lax.psum_scatter(term_sums, 'frames', scatter_dimension=0, tiled=True)]
    ppermute x0 -> x15, waiting for transfers between devices: none -> 5.78 us  [local(): lax.ppermute(sent, 'frames', [(i, i ^ hop) for i in range(count)])]
    unnamed x1, blocking collectives: 64.5 us -> 59.9 us
    unnamed x21 -> x36, local copies, waits for them, and re-layouts: 3.85 us -> 4.67 us
  transfers between devices with their start and end apart: 3 -> 17, of which waited for: 2 -> 4; matrix products, arithmetic and copies ran while one was open for 25% -> 21% of each run, Pallas kernels for 0% -> 0%
where the time goes in v1:
time: 190 us
  blocking collectives  59.9 us (32%)
  matrix products  44.1 us (23%)
  starting transfers between devices  23.6 us (12%)
  waiting for transfers between devices  18.2 us (10%)
  between operations  15.1 us (8%)
  other arithmetic  14.8 us (8%)
  local copies, waits for them, and re-layouts  13.9 us (7%)
    unnamed x1, blocking collectives  59.9 us
    ppermute x15, starting transfers between devices, local(): lax.ppermute(sent, 'frames', [(i, i ^ hop) for i in range(count)])  23.5 us
    dot_general x1, matrix products, local(): lax.dot_general(probs, unit_token_vectors, (((0,), (0,)), ((), ())), prec...  15.1 us
    reduce_scatter x1, waiting for transfers between devices, local(): lax.psum_scatter(term_sums, 'frames', scatter_dimension=0, tiled=True)  12.4 us
    dot_general x1, matrix products, local(): jnp.dot(unit_token_vectors, codebook_matrix.T, precision=TOP_PRECISION)  9.7 us
    ppermute x15, waiting for transfers between devices, local(): lax.ppermute(sent, 'frames', [(i, i ^ hop) for i in range(count)])  5.78 us
    unnamed x36, local copies, waits for them, and re-layouts  4.67 us
    reduce_sum x1, other arithmetic, local(): term_counts = jnp.sum(probs, 0)  4.27 us
  transfers between devices with their start and end apart: 17, of which 4 were waited for; matrix products, arithmetic and copies ran while one was open for 21% of the time, Pallas kernels for 0%

profile of v1, /device:TPU:0, one launch (start us, length us, event | category | flops | bytes accessed | tf_op | source)
XLA Modules:
  0.0 189.7 jit_solution(9925320503380913837)
XLA Ops:
  7.2 1.2 multiply_reduce_fusion.5
  8.4 1.8 broadcast_multiply_fusion.2
  10.4 14.1 %while.10 = (s32[]{:T(128)}, f32[2,256,256]{2,1,0:T(8,128)}, f32[2,256,256]{2,1,0:T(8,128)}, f32[256]{0:T(256)}, f32[256,768]{1,0:T(8,128)}, /*index=5*/f32[256,256]{1,0:T(8,128)}, s32[]{:T(128)}) while((s32[]{:T(128)}, f32[2,256,256]{2,1,0:T(8,128)}, f32[2,256,256]{2,1,0:T(8,128)}, f32[256]{0:T(256)}, f32[256,768]{1,0:T(8,128)}, ...), condition=%wide.region_5.6_spmd, body=%wide.region_0.5_spmd.sunk | while | flops 1209269504 | bytes 13154441 | solution.py:88
  10.4 1.1 fusion.71
  11.6 2.1 %fusion.72 = f32[256,768]{1,0:T(8,128)S(1)} fusion(f32[256,768]{1,0:T(8,128)} %get-tuple-element.155, f32[2,256,256]{2,1,0:T(8,128)} %get-tuple-element.153, s32[]{:T(128)} %get-tuple-element.144, f32[256]{0:T(256)} %get-tuple-element.154, f32[256]{0:T(256)S(1)} %add_rsqrt_fusion.10), kind=kOutput, calls=%fused_computation.12.clone.1 | convolution fusion | flops 604110848 | bytes 1837568 | tf_op jit(solution)/shard_map/while/body/eval_jaxpr/dot_general | solution.py:36
  14.1 1.1 fusion.74
  15.4 0.8 fusion.75
  16.2 1.3 fusion.76
  17.5 1.1 fusion.71
  18.6 2.1 %fusion.72 = f32[256,768]{1,0:T(8,128)S(1)} fusion(f32[256,768]{1,0:T(8,128)} %get-tuple-element.155, f32[2,256,256]{2,1,0:T(8,128)} %get-tuple-element.153, s32[]{:T(128)} %get-tuple-element.144, f32[256]{0:T(256)} %get-tuple-element.154, f32[256]{0:T(256)S(1)} %add_rsqrt_fusion.10), kind=kOutput, calls=%fused_computation.12.clone.1 | convolution fusion | flops 604110848 | bytes 1837568 | tf_op jit(solution)/shard_map/while/body/eval_jaxpr/dot_general | solution.py:36
  21.2 1.1 fusion.74
  22.4 0.8 fusion.75
  23.2 1.3 fusion.76
  24.5 1.0 dynamic-slice_bitcast_fusion
  25.6 0.6 collective-permute-start
  26.1 2.6 %collective-permute-start.1 = (f32[2,1,16,256]{3,2,0,1:T(8,128)S(1)}, f32[2,1,16,256]{3,2,0,1:T(8,128)S(1)}, u32[]{:S(2)}, u32[]{:S(2)}) collective-permute-start(f32[2,1,16,256]{3,2,0,1:T(8,128)S(1)} %get-tuple-element.74), channel_id=1, source_target_pairs={{0,2},{1,3},{2,0},{3,1},{4,6},{5,7},{6,4},{7,5},{8,10},{9,11},{10,... | collective-permute-start | bytes 98312 | tf_op jit(solution)/shard_map/ppermute | solution.py:97
  28.8 1.8 collective-permute-start.3
  30.6 0.8 constant_dynamic-update-slice_fusion.15
  31.5 2.7 %collective-permute-start.5 = (f32[2,1,16,256]{3,2,0,1:T(8,128)S(1)}, f32[2,1,16,256]{3,2,0,1:T(8,128)S(1)}, u32[]{:S(2)}, u32[]{:S(2)}) collective-permute-start(f32[2,1,16,256]{3,2,0,1:T(8,128)S(1)} %get-tuple-element.70), channel_id=1, source_target_pairs={{0,6},{1,7},{2,4},{3,5},{4,2},{5,3},{6,0},{7,1},{8,14},{9,15},{10,... | collective-permute-start | bytes 98312 | tf_op jit(solution)/shard_map/ppermute | solution.py:97
  34.4 2.7 %collective-permute-start.7 = (f32[2,1,16,256]{3,2,0,1:T(8,128)S(1)}, f32[2,1,16,256]{3,2,0,1:T(8,128)S(1)}, u32[]{:S(2)}, u32[]{:S(2)}) collective-permute-start(f32[2,1,16,256]{3,2,0,1:T(8,128)S(1)} %get-tuple-element.68), channel_id=1, source_target_pairs={{0,8},{1,9},{2,10},{3,11},{4,12},{5,13},{6,14},{7,15},{8,0},{9,1},... | collective-permute-start | bytes 98312 | tf_op jit(solution)/shard_map/ppermute | solution.py:97
  37.1 3.5 %collective-permute-start.9 = (f32[2,1,16,256]{3,2,0,1:T(8,128)S(1)}, f32[2,1,16,256]{3,2,0,1:T(8,128)S(1)}, u32[]{:S(2)}, u32[]{:S(2)}) collective-permute-start(f32[2,1,16,256]{3,2,0,1:T(8,128)S(1)} %get-tuple-element.66), channel_id=1, source_target_pairs={{0,10},{1,11},{2,8},{3,9},{4,14},{5,15},{6,12},{7,13},{8,2},{9,3},... | collective-permute-start | bytes 98312 | tf_op jit(solution)/shard_map/ppermute | solution.py:97
  40.7 3.5 %collective-permute-start.11 = (f32[2,1,16,256]{3,2,0,1:T(8,128)S(1)}, f32[2,1,16,256]{3,2,0,1:T(8,128)S(1)}, u32[]{:S(2)}, u32[]{:S(2)}) collective-permute-start(f32[2,1,16,256]{3,2,0,1:T(8,128)S(1)} %get-tuple-element.64), channel_id=1, source_target_pairs={{0,12},{1,13},{2,14},{3,15},{4,8},{5,9},{6,10},{7,11},{8,4},{9,5},... | collective-permute-start | bytes 98312 | tf_op jit(solution)/shard_map/ppermute | solution.py:97
  44.3 4.4 %collective-permute-start.13 = (f32[2,1,16,256]{3,2,0,1:T(8,128)S(1)}, f32[2,1,16,256]{3,2,0,1:T(8,128)S(1)}, u32[]{:S(2)}, u32[]{:S(2)}) collective-permute-start(f32[2,1,16,256]{3,2,0,1:T(8,128)S(1)} %get-tuple-element.62), channel_id=1, source_target_pairs={{0,14},{1,15},{2,12},{3,13},{4,10},{5,11},{6,8},{7,9},{8,6},{9,7},... | collective-permute-start | bytes 98312 | tf_op jit(solution)/shard_map/ppermute | solution.py:97
  48.7 1.4 collective-permute-start.14
  50.1 0.4 collective-permute-done.12
  50.5 2.5 %collective-permute-done.13 = f32[2,1,16,256]{3,2,0,1:T(8,128)S(1)} collective-permute-done((f32[2,1,16,256]{3,2,0,1:T(8,128)S(1)}, f32[2,1,16,256]{3,2,0,1:T(8,128)S(1)}, u32[]{:S(2)}, u32[]{:S(2)}) %collective-permute-start.13) | collective-permute-done | bytes 32800 | tf_op jit(solution)/shard_map/ppermute | solution.py:97
  53.0 2.9 %collective-permute-done.14 = f32[2,1,16,256]{3,2,0,1:T(8,128)S(1)} collective-permute-done((f32[2,1,16,256]{3,2,0,1:T(8,128)S(1)}, f32[2,1,16,256]{3,2,0,1:T(8,128)S(1)}, u32[]{:S(2)}, u32[]{:S(2)}) %collective-permute-start.14) | collective-permute-done | bytes 32800 | tf_op jit(solution)/shard_map/ppermute | solution.py:97
  55.9 0.6 gather_fusion
  56.7 1.5 fusion.24
  58.1 1.2 fusion.41
  59.3 0.5 reshape.207
  59.8 1.5 reshape.206
  61.3 2.5 %reshape.205 = f32[2,16,16,4,64]{4,3,2,1,0:T(4,128)} reshape(f32[2,16,16,256]{3,2,1,0:T(8,128)} %get-tuple-element.58) | data formatting | bytes 1048576 | tf_op jit(solution)/shard_map/reshape | solution.py:54
  63.7 0.6 multiply_reduce_fusion.2
  64.3 0.6 multiply_reduce_fusion.3
  65.1 1.5 broadcast_multiply_fusion
  66.5 3.1 %fusion.42 = (f32[2,16,4,16]{3,2,1,0:T(4,128)S(1)}, f32[2,16,4,16,16]{3,4,2,1,0:T(8,128)S(1)}) fusion(f32[2,16,16]{1,2,0:T(8,128)S(1)} %and_convert_fusion, f32[2,16,16,4,64]{4,3,2,1,0:T(4,128)S(1)} %get-tuple-element.84, f32[2,16,16,4,64]{4,3,2,1,0:T(4,128)S(1)} %get-tuple-element.85), kind=kOutput, calls=%fused_computation.110 | convolution fusion | flops 25262080 | bytes 1189888 | tf_op jit(solution)/shard_map/ctphd,csphd->cphts/dot_general | solution.py:55
  69.7 2.5 %fusion.18 = f32[2,16,16,4,64]{4,1,3,2,0:T(8,128)S(1)} fusion(f32[2,16,4,16,16]{3,4,2,1,0:T(8,128)S(1)} %get-tuple-element.77, f32[2,16,16,4,64]{4,3,2,1,0:T(4,128)S(1)} %copy-done.6, f32[2,16,16,4]{1,3,2,0:T(4,128)S(1)} %bitcast.215), kind=kOutput, calls=%fused_computation.30 | convolution fusion | flops 25296896 | bytes 1187840 | tf_op jit(solution)/shard_map/cphts,csphd->ctphd/dot_general | solution.py:66
  72.6 0.6 reshape.208
  73.3 1.6 multiply_reduce_fusion.4
  75.2 9.7 %fusion.17 = (f32[512]{0:T(512)S(1)}, f32[512,4096]{1,0:T(8,128)S(1)}) fusion(f32[512,256]{1,0:T(8,128)S(1)} %bitcast_multiply_fusion.2, f32[4096,256]{1,0:T(8,128)} %all-gather.2.cloned.1.call-done), kind=kOutput, calls=%fused_computation.28 | convolution fusion | flops 6446644736 | bytes 13109248 | tf_op jit(solution)/shard_map/dot_general | solution.py:105
  84.9 3.2 %copy-done.1 = f32[512,4096]{1,0:T(8,128)} copy-done((f32[512,4096]{1,0:T(8,128)}, f32[512,4096]{1,0:T(8,128)S(1)}, u32[]{:S(2)}) %copy-start.1) | copy-done | bytes 8388632
  88.1 15.1 %fusion.31 = f32[4096,256]{1,0:T(8,128)} fusion(f32[512,256]{1,0:T(8,128)S(1)} %bitcast_multiply_fusion.2, f32[512,4096]{1,0:T(8,128)S(1)} %get-tuple-element.81, f32[512]{0:T(512)S(1)} %get-tuple-element.80), kind=kOutput, calls=%fused_computation.52 | convolution fusion | flops 6446645248 | bytes 13109248 | tf_op jit(solution)/shard_map/dot_general | solution.py:108
  103.2 0.6 dynamic-slice.64
  104.4 4.3 %fusion.30 = f32[4096]{0:T(1024)S(1)} fusion(f32[512]{0:T(512)S(1)} %get-tuple-element.80, f32[512,4096]{1,0:T(8,128)} %copy-done.1), kind=kLoop, calls=%fused_computation.51 | loop fusion | flops 6287360 | bytes 8407040 | tf_op jit(solution)/shard_map/reduce_sum | solution.py:111
  108.7 59.9 %all-reduce = f32[4096]{0:T(1024)S(1)} all-reduce(f32[4096]{0:T(1024)S(1)} %fusion.30), channel_id=3, replica_groups=mesh['groups'=2,'frames'=16] {'frames'}, use_global_device_ids=true, to_apply=%region_15.16.clone | all-reduce | flops 4096 | bytes 32768
  168.7 12.4 %reduce-scatter.2.cloned.1.call-done = f32[256,256]{1,0:T(8,128)} async-done(((f32[4096,256]{1,0:T(8,128)}), f32[256,256]{1,0:T(8,128)}) %reduce-scatter.2.cloned.1.call-update) | async-done | bytes 262160 | tf_op jit(solution)/shard_map/reduce_scatter | solution.py:113
  181.1 1.8 broadcast_divide_fusion
  (97 shorter events, 2.8 us)
Async XLA Ops:
  7.2 49.5 %copy-start = (f32[256,768]{1,0:T(8,128)S(1)}, f32[256,768]{1,0:T(8,128)}, u32[]{:S(2)}) copy-start(f32[256,768]{1,0:T(8,128)} %param.18) | copy-start | bytes 2359300
  7.2 68.0 %all-gather.2.cloned.1.call-start = ((), (), s32[]{:S(2)}) async-start(), calls=%async_computation.1 | async-start | bytes 4456448 | tf_op jit(solution)/shard_map/all_gather | solution.py:103
  10.3 170.8 %reduce-scatter.2.cloned.1.call-start = ((), (), s32[]{:S(2)}) async-start(), calls=%async_computation.2 | async-start | bytes 4456448 | tf_op jit(solution)/shard_map/reduce_scatter | solution.py:113
  10.4 21.0 %copy-start.10 = (s32[2]{0:T(128)S(1)}, s32[2]{0:T(128)}, u32[]{:S(2)}) copy-start(s32[2]{0:T(128)} %param.13) | copy-start | bytes 28
  10.4 46.3 %copy-start.9 = (f32[256]{0:T(256)S(1)}, f32[256]{0:T(256)}, u32[]{:S(2)}) copy-start(f32[256]{0:T(256)} %param.17) | copy-start | bytes 3076
  10.4 5.7 %copy-start.2 = (f32[2,256,256]{2,1,0:T(8,128)S(1)}, f32[2,256,256]{2,1,0:T(8,128)}, u32[]{:S(2)}) copy-start(f32[2,256,256]{2,1,0:T(8,128)} %get-tuple-element.153) | copy-start | bytes 1572868 | tf_op jit(solution)/shard_map/while
  10.4 5.7 %copy-start.3 = (f32[256,256]{1,0:T(8,128)S(1)}, f32[256,256]{1,0:T(8,128)}, u32[]{:S(2)}) copy-start(f32[256,256]{1,0:T(8,128)} %get-tuple-element.156) | copy-start | bytes 786436 | tf_op jit(solution)/shard_map/while
  17.5 5.7 %copy-start.2 = (f32[2,256,256]{2,1,0:T(8,128)S(1)}, f32[2,256,256]{2,1,0:T(8,128)}, u32[]{:S(2)}) copy-start(f32[2,256,256]{2,1,0:T(8,128)} %get-tuple-element.153) | copy-start | bytes 1572868 | tf_op jit(solution)/shard_map/while
  17.5 5.7 %copy-start.3 = (f32[256,256]{1,0:T(8,128)S(1)}, f32[256,256]{1,0:T(8,128)}, u32[]{:S(2)}) copy-start(f32[256,256]{1,0:T(8,128)} %get-tuple-element.156) | copy-start | bytes 786436 | tf_op jit(solution)/shard_map/while
  25.6 6.0 %collective-permute-start = (f32[2,1,16,256]{3,2,0,1:T(8,128)S(1)}, f32[2,1,16,256]{3,2,0,1:T(8,128)S(1)}, u32[]{:S(2)}, u32[]{:S(2)}) collective-permute-start(f32[2,1,16,256]{3,2,0,1:T(8,128)S(1)} %get-tuple-element.75), channel_id=1, source_target_pairs={{0,1},{1,0},{2,3},{3,2},{4,5},{5,4},{6,7},{7,6},{8,9},{9,8},{10,11... | collective-permute-start | bytes 98312 | tf_op jit(solution)/shard_map/ppermute | solution.py:97
  26.1 8.2 %collective-permute-start.1 = (f32[2,1,16,256]{3,2,0,1:T(8,128)S(1)}, f32[2,1,16,256]{3,2,0,1:T(8,128)S(1)}, u32[]{:S(2)}, u32[]{:S(2)}) collective-permute-start(f32[2,1,16,256]{3,2,0,1:T(8,128)S(1)} %get-tuple-element.74), channel_id=1, source_target_pairs={{0,2},{1,3},{2,0},{3,1},{4,6},{5,7},{6,4},{7,5},{8,10},{9,11},{10,... | collective-permute-start | bytes 98312 | tf_op jit(solution)/shard_map/ppermute | solution.py:97
  28.7 5.7 %collective-permute-start.2 = (f32[2,1,16,256]{3,2,0,1:T(8,128)S(1)}, f32[2,1,16,256]{3,2,0,1:T(8,128)S(1)}, u32[]{:S(2)}, u32[]{:S(2)}) collective-permute-start(f32[2,1,16,256]{3,2,0,1:T(8,128)S(1)} %get-tuple-element.73), channel_id=1, source_target_pairs={{0,3},{1,2},{2,1},{3,0},{4,7},{5,6},{6,5},{7,4},{8,11},{9,10},{10,... | collective-permute-start | bytes 98312 | tf_op jit(solution)/shard_map/ppermute | solution.py:97
  28.8 8.3 %collective-permute-start.3 = (f32[2,1,16,256]{3,2,0,1:T(8,128)S(1)}, f32[2,1,16,256]{3,2,0,1:T(8,128)S(1)}, u32[]{:S(2)}, u32[]{:S(2)}) collective-permute-start(f32[2,1,16,256]{3,2,0,1:T(8,128)S(1)} %get-tuple-element.72), channel_id=1, source_target_pairs={{0,4},{1,5},{2,6},{3,7},{4,0},{5,1},{6,2},{7,3},{8,12},{9,13},{10,... | collective-permute-start | bytes 98312 | tf_op jit(solution)/shard_map/ppermute | solution.py:97
  30.6 6.5 %collective-permute-start.4 = (f32[2,1,16,256]{3,2,0,1:T(8,128)S(1)}, f32[2,1,16,256]{3,2,0,1:T(8,128)S(1)}, u32[]{:S(2)}, u32[]{:S(2)}) collective-permute-start(f32[2,1,16,256]{3,2,0,1:T(8,128)S(1)} %get-tuple-element.71), channel_id=1, source_target_pairs={{0,5},{1,4},{2,7},{3,6},{4,1},{5,0},{6,3},{7,2},{8,13},{9,12},{10,... | collective-permute-start | bytes 98312 | tf_op jit(solution)/shard_map/ppermute | solution.py:97
  31.5 9.1 %collective-permute-start.5 = (f32[2,1,16,256]{3,2,0,1:T(8,128)S(1)}, f32[2,1,16,256]{3,2,0,1:T(8,128)S(1)}, u32[]{:S(2)}, u32[]{:S(2)}) collective-permute-start(f32[2,1,16,256]{3,2,0,1:T(8,128)S(1)} %get-tuple-element.70), channel_id=1, source_target_pairs={{0,6},{1,7},{2,4},{3,5},{4,2},{5,3},{6,0},{7,1},{8,14},{9,15},{10,... | collective-permute-start | bytes 98312 | tf_op jit(solution)/shard_map/ppermute | solution.py:97
  34.3 6.5 %collective-permute-start.6 = (f32[2,1,16,256]{3,2,0,1:T(8,128)S(1)}, f32[2,1,16,256]{3,2,0,1:T(8,128)S(1)}, u32[]{:S(2)}, u32[]{:S(2)}) collective-permute-start(f32[2,1,16,256]{3,2,0,1:T(8,128)S(1)} %get-tuple-element.69), channel_id=1, source_target_pairs={{0,7},{1,6},{2,5},{3,4},{4,3},{5,2},{6,1},{7,0},{8,15},{9,14},{10,... | collective-permute-start | bytes 98312 | tf_op jit(solution)/shard_map/ppermute | solution.py:97
  34.4 9.9 %collective-permute-start.7 = (f32[2,1,16,256]{3,2,0,1:T(8,128)S(1)}, f32[2,1,16,256]{3,2,0,1:T(8,128)S(1)}, u32[]{:S(2)}, u32[]{:S(2)}) collective-permute-start(f32[2,1,16,256]{3,2,0,1:T(8,128)S(1)} %get-tuple-element.68), channel_id=1, source_target_pairs={{0,8},{1,9},{2,10},{3,11},{4,12},{5,13},{6,14},{7,15},{8,0},{9,1},... | collective-permute-start | bytes 98312 | tf_op jit(solution)/shard_map/ppermute | solution.py:97
  37.1 7.3 %collective-permute-start.8 = (f32[2,1,16,256]{3,2,0,1:T(8,128)S(1)}, f32[2,1,16,256]{3,2,0,1:T(8,128)S(1)}, u32[]{:S(2)}, u32[]{:S(2)}) collective-permute-start(f32[2,1,16,256]{3,2,0,1:T(8,128)S(1)} %get-tuple-element.67), channel_id=1, source_target_pairs={{0,9},{1,8},{2,11},{3,10},{4,13},{5,12},{6,15},{7,14},{8,1},{9,0},... | collective-permute-start | bytes 98312 | tf_op jit(solution)/shard_map/ppermute | solution.py:97
  37.1 11.6 %collective-permute-start.9 = (f32[2,1,16,256]{3,2,0,1:T(8,128)S(1)}, f32[2,1,16,256]{3,2,0,1:T(8,128)S(1)}, u32[]{:S(2)}, u32[]{:S(2)}) collective-permute-start(f32[2,1,16,256]{3,2,0,1:T(8,128)S(1)} %get-tuple-element.66), channel_id=1, source_target_pairs={{0,10},{1,11},{2,8},{3,9},{4,14},{5,15},{6,12},{7,13},{8,2},{9,3},... | collective-permute-start | bytes 98312 | tf_op jit(solution)/shard_map/ppermute | solution.py:97
  40.6 9.5 %collective-permute-start.10 = (f32[2,1,16,256]{3,2,0,1:T(8,128)S(1)}, f32[2,1,16,256]{3,2,0,1:T(8,128)S(1)}, u32[]{:S(2)}, u32[]{:S(2)}) collective-permute-start(f32[2,1,16,256]{3,2,0,1:T(8,128)S(1)} %get-tuple-element.65), channel_id=1, source_target_pairs={{0,11},{1,10},{2,9},{3,8},{4,15},{5,14},{6,13},{7,12},{8,3},{9,2},... | collective-permute-start | bytes 98312 | tf_op jit(solution)/shard_map/ppermute | solution.py:97
  40.7 9.4 %collective-permute-start.11 = (f32[2,1,16,256]{3,2,0,1:T(8,128)S(1)}, f32[2,1,16,256]{3,2,0,1:T(8,128)S(1)}, u32[]{:S(2)}, u32[]{:S(2)}) collective-permute-start(f32[2,1,16,256]{3,2,0,1:T(8,128)S(1)} %get-tuple-element.64), channel_id=1, source_target_pairs={{0,12},{1,13},{2,14},{3,15},{4,8},{5,9},{6,10},{7,11},{8,4},{9,5},... | collective-permute-start | bytes 98312 | tf_op jit(solution)/shard_map/ppermute | solution.py:97
  44.3 6.3 %collective-permute-start.12 = (f32[2,1,16,256]{3,2,0,1:T(8,128)S(1)}, f32[2,1,16,256]{3,2,0,1:T(8,128)S(1)}, u32[]{:S(2)}, u32[]{:S(2)}) collective-permute-start(f32[2,1,16,256]{3,2,0,1:T(8,128)S(1)} %get-tuple-element.63), channel_id=1, source_target_pairs={{0,13},{1,12},{2,15},{3,14},{4,9},{5,8},{6,11},{7,10},{8,5},{9,4},... | collective-permute-start | bytes 98312 | tf_op jit(solution)/shard_map/ppermute | solution.py:97
  44.3 8.7 %collective-permute-start.13 = (f32[2,1,16,256]{3,2,0,1:T(8,128)S(1)}, f32[2,1,16,256]{3,2,0,1:T(8,128)S(1)}, u32[]{:S(2)}, u32[]{:S(2)}) collective-permute-start(f32[2,1,16,256]{3,2,0,1:T(8,128)S(1)} %get-tuple-element.62), channel_id=1, source_target_pairs={{0,14},{1,15},{2,12},{3,13},{4,10},{5,11},{6,8},{7,9},{8,6},{9,7},... | collective-permute-start | bytes 98312 | tf_op jit(solution)/shard_map/ppermute | solution.py:97
  48.7 7.2 %collective-permute-start.14 = (f32[2,1,16,256]{3,2,0,1:T(8,128)S(1)}, f32[2,1,16,256]{3,2,0,1:T(8,128)S(1)}, u32[]{:S(2)}, u32[]{:S(2)}) collective-permute-start(f32[2,1,16,256]{3,2,0,1:T(8,128)S(1)} %get-tuple-element.61), channel_id=1, source_target_pairs={{0,15},{1,14},{2,13},{3,12},{4,11},{5,10},{6,9},{7,8},{8,7},{9,6},... | collective-permute-start | bytes 98312 | tf_op jit(solution)/shard_map/ppermute | solution.py:97
  63.7 6.0 %copy-start.6 = (f32[2,16,16,4,64]{4,3,2,1,0:T(4,128)S(1)}, f32[2,16,16,4,64]{4,3,2,1,0:T(4,128)}, u32[]{:S(2)}) copy-start(f32[2,16,16,4,64]{4,3,2,1,0:T(4,128)} %reshape.205) | copy-start | bytes 1572868
  74.9 28.3 %copy-start.5 = (f32[2,16,16,256]{3,2,1,0:T(8,128)}, f32[2,16,16,256]{3,2,1,0:T(8,128)S(1)}, u32[]{:S(2)}) copy-start(f32[2,16,16,256]{3,2,1,0:T(8,128)S(1)} %get-tuple-element.79) | copy-start | bytes 1572868
  84.9 3.2 %copy-start.1 = (f32[512,4096]{1,0:T(8,128)}, f32[512,4096]{1,0:T(8,128)S(1)}, u32[]{:S(2)}) copy-start(f32[512,4096]{1,0:T(8,128)S(1)} %get-tuple-element.81) | copy-start | bytes 25165828
  88.1 15.1 %copy-start.11 = (u32[32]{0:T(128)S(1)}, u32[32]{0:T(128)}, u32[]{:S(2)}) copy-start(u32[32]{0:T(128)} %constant.37) | copy-start | bytes 388
  103.1 65.5 %copy-start.7 = (f32[256]{0:T(256)S(1)}, f32[256]{0:T(256)}, u32[]{:S(2)}) copy-start(f32[256]{0:T(256)} %param.21) | copy-start | bytes 3076
  103.1 78.0 %copy-start.4 = (f32[256,256]{1,0:T(8,128)S(1)}, f32[256,256]{1,0:T(8,128)}, u32[]{:S(2)}) copy-start(f32[256,256]{1,0:T(8,128)} %param.20) | copy-start | bytes 786436
  168.7 14.2 %copy-start.8 = (f32[256]{0:T(256)}, f32[256]{0:T(256)S(1)}, u32[]{:S(2)}) copy-start(f32[256]{0:T(256)S(1)} %fusion.36) | copy-start | bytes 3076
Sparse Core Ops, SparseCore 0:
  10.7 58.7 all-gather.1
  103.3 77.7 reduce-scatter.1
